TPU v7x, 256 devices: a whole 4x4x8 slice. The times are simulated.
256 devices in a mesh: prow: 8 (over z), pcol: 32 (over x, y, core).
Axes of the slice: x: 4, y: 4, z: 8, core: 2. Of those that a mesh axis runs over, the one named last changes fastest.
Arguments:
- matrix: bfloat16 [8, 2048, 2, 8192], P(None, 'prow', None, 'pcol'), may hold values from -6 to 6
- pivots: int32 [4, 256], replicated, may hold values from 0 to 16383, as said below
- lower_inverse: bfloat16 [4, 256, 256], replicated, as said below
- upper_inverse: bfloat16 [4, 256, 256], replicated, as said below
Outputs:
- factored: bfloat16 [8, 2048, 2, 8192], P(None, 'prow', None, 'pcol')
Inputs may be any that keep to these rules, and one draw needn't show every extreme that they name: For step s and each i, pivots[s, i] is either s * 256 + i or a row index of s * 256 + 256 or more; the pivots of one step that differ from s * 256 + i are distinct. lower_inverse[s] is unit lower triangular. upper_inverse[s] is upper triangular.
All inputs are finite; a program needn't handle non-finite values.
Results may differ from a plain program's by a relative error of at most 0.0071.
Values may be sent and summed in bfloat16 or wider, within the bound.
A program may use at most 64 MiB of HBM per device.

v0:
```python
import jax
import jax.numpy as jnp
from jax import lax
from jax.sharding import PartitionSpec as P


def spread(value, axis, source):
    kept = jnp.where(lax.axis_index(axis) == source, value, 0).astype(value.dtype)
    return lax.psum(kept, axis)


def local(matrix, pivots, lower_inverse, upper_inverse):
    row_blocks = matrix.shape[0]
    block_size = matrix.shape[1]
    col_blocks = matrix.shape[2]
    local_rows = row_blocks * block_size
    local_cols = col_blocks * block_size
    matrix_loc = matrix.reshape(local_rows, local_cols)
    row_count = lax.axis_size("prow")
    col_count = lax.axis_size("pcol")
    my_row = lax.axis_index("prow")
    my_col = lax.axis_index("pcol")
    row_iota = jnp.arange(local_rows, dtype=jnp.int32)
    col_iota = jnp.arange(local_cols, dtype=jnp.int32)
    global_row = (row_iota // block_size * row_count + my_row) * block_size + row_iota % block_size
    global_col = (col_iota // block_size * col_count + my_col) * block_size + col_iota % block_size
    for step_num in range(pivots.shape[0]):
        begin_at = step_num * block_size
        trail_at = begin_at + block_size
        diag_root = step_num % row_count
        diag_local = step_num // row_count * block_size
        panel_root = step_num % col_count
        panel_local = step_num // col_count * block_size
        targets = begin_at + jnp.arange(block_size, dtype=jnp.int32)
        chosen = pivots[step_num]
        chosen_block = chosen // block_size
        chosen_owner = chosen_block % row_count
        is_mine = chosen_owner == my_row
        chosen_local = chosen_block // row_count * block_size + chosen % block_size
        picked = jnp.take(matrix_loc, jnp.where(is_mine, chosen_local, 0), axis=0)
        picked = jnp.where(is_mine[:, None], picked, jnp.zeros_like(picked))
        diag_rows = matrix_loc[diag_local : diag_local + block_size]
        gathered = lax.all_gather(picked, "prow", axis=0, tiled=True)
        stacked = gathered.reshape(row_count, block_size, local_cols)
        owner_hit = jnp.arange(row_count, dtype=jnp.int32)[:, None] == chosen_owner[None, :]
        new_rows = jnp.sum(
            jnp.where(owner_hit[:, :, None], stacked, jnp.zeros_like(stacked)), axis=0
        )
        old_diag = spread(diag_rows, "prow", diag_root)
        moved_rows = is_mine & (chosen != targets)
        matrix_loc = matrix_loc.at[jnp.where(moved_rows, chosen_local, local_rows)].set(
            old_diag, mode="drop"
        )
        diag_after = matrix_loc[diag_local : diag_local + block_size]
        matrix_loc = matrix_loc.at[diag_local : diag_local + block_size].set(
            jnp.where(my_row == diag_root, new_rows, diag_after)
        )
        upper_full = jnp.dot(
            lower_inverse[step_num], new_rows, preferred_element_type=jnp.float32
        ).astype(jnp.bfloat16)
        col_live = global_col >= trail_at
        upper_use = jnp.where(col_live[None, :], upper_full, jnp.zeros_like(upper_full))
        panel_own = matrix_loc[:, panel_local : panel_local + block_size]
        received = spread(panel_own, "pcol", panel_root)
        left_full = jnp.dot(
            received, upper_inverse[step_num], preferred_element_type=jnp.float32
        ).astype(jnp.bfloat16)
        row_live = global_row >= trail_at
        left_use = jnp.where(row_live[:, None], left_full, jnp.zeros_like(left_full))
        matrix_loc = (
            matrix_loc.astype(jnp.float32)
            - jnp.dot(left_use, upper_use, preferred_element_type=jnp.float32)
        ).astype(jnp.bfloat16)
        panel_now = matrix_loc[:, panel_local : panel_local + block_size]
        panel_put = jnp.where(row_live[:, None] & (my_col == panel_root), left_full, panel_now)
        matrix_loc = matrix_loc.at[:, panel_local : panel_local + block_size].set(panel_put)
        diag_now = matrix_loc[diag_local : diag_local + block_size]
        diag_put = jnp.where(col_live[None, :] & (my_row == diag_root), upper_full, diag_now)
        matrix_loc = matrix_loc.at[diag_local : diag_local + block_size].set(diag_put)
    return matrix_loc.reshape(matrix.shape)


def solution(mesh):
    placed = (P(None, "prow", None, "pcol"), P(), P(), P())
    return jax.shard_map(
        local, mesh=mesh, in_specs=placed, out_specs=P(None, "prow", None, "pcol"), check_vma=False
    )
```

profile of v0, /device:TPU:1, one launch (start us, length us, event | category | flops | bytes accessed | tf_op | source)
XLA Modules:
  0.0 982.3 jit_solution(12199594610326055330)
XLA Ops:
  6.5 1.2 broadcast_select_fusion
  8.5 0.9 and_select_fusion
  9.4 2.0 copy.17
  11.5 1.2 gather_fusion
  14.4 66.9 %all-reduce.9.cloned.1.call-done = bf16[256,512]{1,0:T(8,128)(2,1)} async-done(((bf16[256,512]{1,0:T(8,128)(2,1)}), bf16[256,512]{1,0:T(8,128)(2,1)}) %all-reduce.9.cloned.1.call-update) | async-done | bytes 262160 | tf_op jit(solution)/shard_map/psum | solution.py:9
  81.3 3.1 scatter_fusion
  84.4 38.9 %all-gather.5.cloned.1.call-done = bf16[2048,512]{1,0:T(8,128)(2,1)} async-done(((bf16[256,512]{1,0:T(8,128)(2,1)}), bf16[2048,512]{1,0:T(8,128)(2,1)}) %all-gather.5.cloned.1.call-update) | async-done | bytes 2097168 | tf_op jit(solution)/shard_map/all_gather | solution.py:43
  123.4 1.9 select_reduce_fusion.3
  125.3 1.0 slice_select_fusion.3
  126.7 118.0 %all-reduce.11.cloned.1.call-done = bf16[2048,256]{1,0:T(8,128)(2,1)} async-done(((bf16[2048,256]{1,0:T(8,128)(2,1)}), bf16[2048,256]{1,0:T(8,128)(2,1)}) %all-reduce.11.cloned.1.call-update) | async-done | bytes 1048592 | tf_op jit(solution)/shard_map/psum | solution.py:9
  244.7 1.6 convolution_convert_fusion.3
  246.4 2.0 subtract_convert_fusion.3
  248.4 3.4 fusion.4
  251.8 1.8 broadcast_select_fusion.3
  253.7 3.1 gather_fusion.1
  257.8 63.7 %all-reduce.13.cloned.1.call-done = bf16[256,512]{1,0:T(8,128)(2,1)} async-done(((bf16[256,512]{1,0:T(8,128)(2,1)}), bf16[256,512]{1,0:T(8,128)(2,1)}) %all-reduce.13.cloned.1.call-update) | async-done | bytes 262160 | tf_op jit(solution)/shard_map/psum | solution.py:9
  321.5 5.2 scatter_fusion.1
  326.7 36.7 %all-gather.7.cloned.1.call-done = bf16[2048,512]{1,0:T(8,128)(2,1)} async-done(((bf16[256,512]{1,0:T(8,128)(2,1)}), bf16[2048,512]{1,0:T(8,128)(2,1)}) %all-gather.7.cloned.1.call-update) | async-done | bytes 2097168 | tf_op jit(solution)/shard_map/all_gather | solution.py:43
  363.4 1.9 select_reduce_fusion.2
  365.2 1.7 fusion.23
  367.0 2.3 slice_select_fusion.2
  369.6 118.0 %all-reduce.15.cloned.1.call-done = bf16[2048,256]{1,0:T(8,128)(2,1)} async-done(((bf16[2048,256]{1,0:T(8,128)(2,1)}), bf16[2048,256]{1,0:T(8,128)(2,1)}) %all-reduce.15.cloned.1.call-update) | async-done | bytes 1048592 | tf_op jit(solution)/shard_map/psum | solution.py:9
  487.6 1.6 convolution_convert_fusion.2
  489.3 2.3 subtract_convert_fusion.2
  491.5 1.5 fusion.5
  494.1 1.2 gather_fusion.2
  496.2 65.4 %all-reduce.17.cloned.1.call-done = bf16[256,512]{1,0:T(8,128)(2,1)} async-done(((bf16[256,512]{1,0:T(8,128)(2,1)}), bf16[256,512]{1,0:T(8,128)(2,1)}) %all-reduce.17.cloned.1.call-update) | async-done | bytes 262160 | tf_op jit(solution)/shard_map/psum | solution.py:9
  561.6 3.1 scatter_fusion.2
  564.7 38.9 %all-gather.9.cloned.1.call-done = bf16[2048,512]{1,0:T(8,128)(2,1)} async-done(((bf16[256,512]{1,0:T(8,128)(2,1)}), bf16[2048,512]{1,0:T(8,128)(2,1)}) %all-gather.9.cloned.1.call-update) | async-done | bytes 2097168 | tf_op jit(solution)/shard_map/all_gather | solution.py:43
  603.6 1.9 select_reduce_fusion.1
  605.6 1.0 slice_select_fusion.1
  607.0 118.0 %all-reduce.19.cloned.1.call-done = bf16[2048,256]{1,0:T(8,128)(2,1)} async-done(((bf16[2048,256]{1,0:T(8,128)(2,1)}), bf16[2048,256]{1,0:T(8,128)(2,1)}) %all-reduce.19.cloned.1.call-update) | async-done | bytes 1048592 | tf_op jit(solution)/shard_map/psum | solution.py:9
  725.0 1.7 convolution_convert_fusion.1
  726.6 2.0 subtract_convert_fusion.1
  728.6 3.4 fusion.6
  732.0 1.8 broadcast_select_fusion.1
  734.0 3.1 gather_fusion.3
  738.0 63.7 %all-reduce.21.cloned.1.call-done = bf16[256,512]{1,0:T(8,128)(2,1)} async-done(((bf16[256,512]{1,0:T(8,128)(2,1)}), bf16[256,512]{1,0:T(8,128)(2,1)}) %all-reduce.21.cloned.1.call-update) | async-done | bytes 262160 | tf_op jit(solution)/shard_map/psum | solution.py:9
  801.7 5.2 scatter_fusion.3
  806.9 36.8 %all-gather.11.cloned.1.call-done = bf16[2048,512]{1,0:T(8,128)(2,1)} async-done(((bf16[256,512]{1,0:T(8,128)(2,1)}), bf16[2048,512]{1,0:T(8,128)(2,1)}) %all-gather.11.cloned.1.call-update) | async-done | bytes 2097168 | tf_op jit(solution)/shard_map/all_gather | solution.py:43
  843.8 1.9 select_reduce_fusion
  845.6 1.7 fusion.21
  847.4 2.3 slice_select_fusion
  850.0 118.0 %all-reduce.23.cloned.1.call-done = bf16[2048,256]{1,0:T(8,128)(2,1)} async-done(((bf16[2048,256]{1,0:T(8,128)(2,1)}), bf16[2048,256]{1,0:T(8,128)(2,1)}) %all-reduce.23.cloned.1.call-update) | async-done | bytes 1048592 | tf_op jit(solution)/shard_map/psum | solution.py:9
  968.0 1.6 convolution_convert_fusion
  969.7 2.3 subtract_convert_fusion
  971.9 1.5 fusion.7
  973.5 2.0 reshape.1320
  (69 shorter events, 8.0 us)
Async XLA Ops:
  6.5 74.8 %all-reduce.9.cloned.1.call-start = ((), (), s32[]{:S(2)}) async-start(), calls=%async_computation | async-start | bytes 524288 | tf_op jit(solution)/shard_map/psum | solution.py:9
  8.5 114.9 %all-gather.5.cloned.1.call-start = ((), (), s32[]{:S(2)}) async-start(), calls=%async_computation.1 | async-start | bytes 2359296 | tf_op jit(solution)/shard_map/all_gather | solution.py:43
  11.5 2.8 copy-start.1
  13.5 231.2 %all-reduce.11.cloned.1.call-start = ((), (), s32[]{:S(2)}) async-start(), calls=%async_computation.2 | async-start | bytes 2097152 | tf_op jit(solution)/shard_map/psum | solution.py:9
  125.2 1.3 copy-start
  126.4 195.1 %all-reduce.13.cloned.1.call-start = ((), (), s32[]{:S(2)}) async-start(), calls=%async_computation.3 | async-start | bytes 524288 | tf_op jit(solution)/shard_map/psum | solution.py:9
  253.6 109.7 %all-gather.7.cloned.1.call-start = ((), (), s32[]{:S(2)}) async-start(), calls=%async_computation.4 | async-start | bytes 2359296 | tf_op jit(solution)/shard_map/all_gather | solution.py:43
  257.6 230.0 %all-reduce.15.cloned.1.call-start = ((), (), s32[]{:S(2)}) async-start(), calls=%async_computation.5 | async-start | bytes 2097152 | tf_op jit(solution)/shard_map/psum | solution.py:9
  369.3 192.3 %all-reduce.17.cloned.1.call-start = ((), (), s32[]{:S(2)}) async-start(), calls=%async_computation.6 | async-start | bytes 524288 | tf_op jit(solution)/shard_map/psum | solution.py:9
  493.8 109.8 %all-gather.9.cloned.1.call-start = ((), (), s32[]{:S(2)}) async-start(), calls=%async_computation.7 | async-start | bytes 2359296 | tf_op jit(solution)/shard_map/all_gather | solution.py:43
  496.1 228.9 %all-reduce.19.cloned.1.call-start = ((), (), s32[]{:S(2)}) async-start(), calls=%async_computation.8 | async-start | bytes 2097152 | tf_op jit(solution)/shard_map/psum | solution.py:9
  606.7 195.1 %all-reduce.21.cloned.1.call-start = ((), (), s32[]{:S(2)}) async-start(), calls=%async_computation.9 | async-start | bytes 524288 | tf_op jit(solution)/shard_map/psum | solution.py:9
  733.9 109.9 %all-gather.11.cloned.1.call-start = ((), (), s32[]{:S(2)}) async-start(), calls=%async_computation.10 | async-start | bytes 2359296 | tf_op jit(solution)/shard_map/all_gather | solution.py:43
  737.9 230.1 %all-reduce.23.cloned.1.call-start = ((), (), s32[]{:S(2)}) async-start(), calls=%async_computation.11 | async-start | bytes 2097152 | tf_op jit(solution)/shard_map/psum | solution.py:9
Sparse Core Ops, SparseCore 0:
  9.6 71.6 all-reduce.8
  83.1 40.1 all-gather.4
  126.6 118.0 all-reduce.10
  253.8 67.6 all-reduce.12
  323.1 40.1 all-gather.6
  369.4 118.1 all-reduce.14
  494.0 67.5 all-reduce.16
  563.4 40.1 all-gather.8
  606.9 118.0 all-reduce.18
  734.0 67.6 all-reduce.20
  803.5 40.1 all-gather.10
  849.8 118.1 all-reduce.22
where the time goes:
time: 983 us; the launch traced here: 982 us
  waiting for transfers between devices  883 us (90%)
  other arithmetic  38.6 us (4%)
  local copies, waits for them, and re-layouts  29.8 us (3%)
  matrix products  16 us (2%)
  between operations  13.9 us (1%)
    psum x8, waiting for transfers between devices, spread(): return lax.psum(kept, axis)  732 us
    all_gather x4, waiting for transfers between devices, local(): gathered = lax.all_gather(picked, 'prow', axis=0, tiled=True)  151 us
  transfers between devices with their start and end apart: 12, of which 12 were waited for; matrix products, arithmetic and copies ran while one was open for 3% of the time, Pallas kernels for 0%

commit v1 on v0

--- a/solution.py
+++ b/solution.py
@@ -40,7 +40,9 @@
         picked = jnp.take(matrix_loc, jnp.where(is_mine, chosen_local, 0), axis=0)
         picked = jnp.where(is_mine[:, None], picked, jnp.zeros_like(picked))
         diag_rows = matrix_loc[diag_local : diag_local + block_size]
-        gathered = lax.all_gather(picked, "prow", axis=0, tiled=True)
+        gathered = jnp.concatenate(
+            lax.all_to_all(jnp.stack([picked] * lax.axis_size("prow")), "prow", 0, 0), axis=0
+        )
         stacked = gathered.reshape(row_count, block_size, local_cols)
         owner_hit = jnp.arange(row_count, dtype=jnp.int32)[:, None] == chosen_owner[None, :]
         new_rows = jnp.sum(

time: 983 us -> 939 us (0.955)
  waiting for transfers between devices: 883 us -> 809 us
  starting transfers between devices: 0.64 us -> 29.7 us
    all_gather x4 -> x0, waiting for transfers between devices: 151 us -> none  [local(): gathered = lax.all_gather(picked, 'prow', axis=0, tiled=True)]
    psum x8, waiting for transfers between devices: 732 us -> 807 us  [spread(): return lax.psum(kept, axis)]
    all_to_all x0 -> x4, starting transfers between devices: none -> 29.3 us  [local(): lax.all_to_all(jnp.stack([picked] * lax.axis_size('prow')), 'prow', 0, 0)]
  transfers between devices with their start and end apart: 12 -> 12, of which waited for: 12 -> 8; matrix products, arithmetic and copies ran while one was open for 3% -> 2% of each run, Pallas kernels for 0% -> 0%
where the time goes in v1:
time: 939 us; the launch traced here: 938 us
  waiting for transfers between devices  809 us (86%)
  local copies, waits for them, and re-layouts  35.9 us (4%)
  other arithmetic  33 us (4%)
  starting transfers between devices  29.7 us (3%)
  matrix products  16 us (2%)
  between operations  13.9 us (1%)
    psum x8, waiting for transfers between devices, spread(): return lax.psum(kept, axis)  807 us
    all_to_all x4, starting transfers between devices, local(): lax.all_to_all(jnp.stack([picked] * lax.axis_size('prow')), 'prow', 0, 0)  29.3 us
  transfers between devices with their start and end apart: 12, of which 8 were waited for; matrix products, arithmetic and copies ran while one was open for 2% of the time, Pallas kernels for 0%

profile of v1, /device:TPU:1, one launch (start us, length us, event | category | flops | bytes accessed | tf_op | source)
XLA Modules:
  0.0 937.8 jit_solution(4130637239781943972)
XLA Ops:
  7.5 2.0 copy.21
  9.5 1.2 gather_fusion
  10.8 1.5 stack.8
  12.3 9.1 all-to-all-start
  21.5 1.2 broadcast_select_fusion
  24.3 82.9 %all-reduce.9.cloned.1.call-done = bf16[256,512]{1,0:T(8,128)(2,1)} async-done(((bf16[256,512]{1,0:T(8,128)(2,1)}), bf16[256,512]{1,0:T(8,128)(2,1)}) %all-reduce.9.cloned.1.call-update) | async-done | bytes 262160 | tf_op jit(solution)/shard_map/psum | solution.py:9
  107.2 3.1 scatter_fusion
  110.3 1.9 select_reduce_fusion.3
  112.3 1.0 slice_select_fusion.3
  113.6 118.8 %all-reduce.11.cloned.1.call-done = bf16[2048,256]{1,0:T(8,128)(2,1)} async-done(((bf16[2048,256]{1,0:T(8,128)(2,1)}), bf16[2048,256]{1,0:T(8,128)(2,1)}) %all-reduce.11.cloned.1.call-update) | async-done | bytes 1048592 | tf_op jit(solution)/shard_map/psum | solution.py:9
  232.4 1.7 convolution_convert_fusion.3
  234.1 2.0 subtract_convert_fusion.3
  236.1 3.4 fusion.4
  239.4 1.9 broadcast_select_fusion.3
  241.3 3.1 gather_fusion.1
  244.5 1.5 stack.9
  246.0 6.7 all-to-all-start.1
  253.6 83.1 %all-reduce.13.cloned.1.call-done = bf16[256,512]{1,0:T(8,128)(2,1)} async-done(((bf16[256,512]{1,0:T(8,128)(2,1)}), bf16[256,512]{1,0:T(8,128)(2,1)}) %all-reduce.13.cloned.1.call-update) | async-done | bytes 262160 | tf_op jit(solution)/shard_map/psum | solution.py:9
  336.7 5.2 scatter_fusion.1
  342.5 1.7 fusion.23
  344.2 2.3 slice_select_fusion.2
  346.8 118.7 %all-reduce.15.cloned.1.call-done = bf16[2048,256]{1,0:T(8,128)(2,1)} async-done(((bf16[2048,256]{1,0:T(8,128)(2,1)}), bf16[2048,256]{1,0:T(8,128)(2,1)}) %all-reduce.15.cloned.1.call-update) | async-done | bytes 1048592 | tf_op jit(solution)/shard_map/psum | solution.py:9
  465.5 1.6 convolution_convert_fusion.2
  467.2 2.3 subtract_convert_fusion.2
  469.5 1.4 fusion.5
  471.7 1.2 gather_fusion.2
  473.0 1.5 stack.10
  474.5 6.7 all-to-all-start.2
  481.9 83.3 %all-reduce.17.cloned.1.call-done = bf16[256,512]{1,0:T(8,128)(2,1)} async-done(((bf16[256,512]{1,0:T(8,128)(2,1)}), bf16[256,512]{1,0:T(8,128)(2,1)}) %all-reduce.17.cloned.1.call-update) | async-done | bytes 262160 | tf_op jit(solution)/shard_map/psum | solution.py:9
  565.2 3.1 scatter_fusion.2
  568.4 1.9 select_reduce_fusion.1
  571.7 118.7 %all-reduce.19.cloned.1.call-done = bf16[2048,256]{1,0:T(8,128)(2,1)} async-done(((bf16[2048,256]{1,0:T(8,128)(2,1)}), bf16[2048,256]{1,0:T(8,128)(2,1)}) %all-reduce.19.cloned.1.call-update) | async-done | bytes 1048592 | tf_op jit(solution)/shard_map/psum | solution.py:9
  690.4 1.7 convolution_convert_fusion.1
  692.0 2.0 subtract_convert_fusion.1
  694.0 3.4 fusion.6
  697.4 1.9 broadcast_select_fusion.1
  699.2 3.1 gather_fusion.3
  702.5 1.5 stack.11
  704.0 6.7 all-to-all-start.3
  711.6 83.1 %all-reduce.21.cloned.1.call-done = bf16[256,512]{1,0:T(8,128)(2,1)} async-done(((bf16[256,512]{1,0:T(8,128)(2,1)}), bf16[256,512]{1,0:T(8,128)(2,1)}) %all-reduce.21.cloned.1.call-update) | async-done | bytes 262160 | tf_op jit(solution)/shard_map/psum | solution.py:9
  794.6 5.2 scatter_fusion.3
  800.4 1.7 fusion.21
  802.2 2.3 slice_select_fusion
  804.8 118.7 %all-reduce.23.cloned.1.call-done = bf16[2048,256]{1,0:T(8,128)(2,1)} async-done(((bf16[2048,256]{1,0:T(8,128)(2,1)}), bf16[2048,256]{1,0:T(8,128)(2,1)}) %all-reduce.23.cloned.1.call-update) | async-done | bytes 1048592 | tf_op jit(solution)/shard_map/psum | solution.py:9
  923.5 1.7 convolution_convert_fusion
  925.2 2.2 subtract_convert_fusion
  927.4 1.4 fusion.7
  928.9 2.0 reshape.1312
  (68 shorter events, 9.6 us)
Async XLA Ops:
  12.3 11.9 %copy-start.1 = (s32[4,256]{1,0:T(4,128)S(1)}, s32[4,256]{1,0:T(4,128)}, u32[]{:S(2)}) copy-start(s32[4,256]{1,0:T(4,128)} %param.31) | copy-start | bytes 12292
  12.3 98.0 %all-to-all-start = ((bf16[8,256,512]{2,1,0:T(8,128)(2,1)}), bf16[8,256,512]{2,1,0:T(8,128)(2,1)}, u32[]{:S(2)}, u32[]{:S(2)}) async-start(bf16[8,256,512]{2,1,0:T(8,128)(2,1)} %stack.8), calls=%async_computation | async-start | bytes 4194304 | tf_op jit(solution)/shard_map/all_to_all | solution.py:44
  21.4 85.8 %all-reduce.9.cloned.1.call-start = ((), (), s32[]{:S(2)}) async-start(), calls=%async_computation.4 | async-start | bytes 524288 | tf_op jit(solution)/shard_map/psum | solution.py:9
  23.4 209.0 %all-reduce.11.cloned.1.call-start = ((), (), s32[]{:S(2)}) async-start(), calls=%async_computation.5 | async-start | bytes 2097152 | tf_op jit(solution)/shard_map/psum | solution.py:9
  112.2 1.2 copy-start
  246.0 95.8 %all-to-all-start.1 = ((bf16[8,256,512]{2,1,0:T(8,128)(2,1)}), bf16[8,256,512]{2,1,0:T(8,128)(2,1)S(1)}, u32[]{:S(2)}, u32[]{:S(2)}) async-start(bf16[8,256,512]{2,1,0:T(8,128)(2,1)} %stack.9), calls=%async_computation.1 | async-start | bytes 4194304 | tf_op jit(solution)/shard_map/all_to_all | solution.py:44
  252.8 83.9 %all-reduce.13.cloned.1.call-start = ((), (), s32[]{:S(2)}) async-start(), calls=%async_computation.6 | async-start | bytes 524288 | tf_op jit(solution)/shard_map/psum | solution.py:9
  253.5 212.0 %all-reduce.15.cloned.1.call-start = ((), (), s32[]{:S(2)}) async-start(), calls=%async_computation.7 | async-start | bytes 2097152 | tf_op jit(solution)/shard_map/psum | solution.py:9
  474.5 93.8 %all-to-all-start.2 = ((bf16[8,256,512]{2,1,0:T(8,128)(2,1)}), bf16[8,256,512]{2,1,0:T(8,128)(2,1)}, u32[]{:S(2)}, u32[]{:S(2)}) async-start(bf16[8,256,512]{2,1,0:T(8,128)(2,1)} %stack.10), calls=%async_computation.2 | async-start | bytes 4194304 | tf_op jit(solution)/shard_map/all_to_all | solution.py:44
  481.3 84.0 %all-reduce.17.cloned.1.call-start = ((), (), s32[]{:S(2)}) async-start(), calls=%async_computation.8 | async-start | bytes 524288 | tf_op jit(solution)/shard_map/psum | solution.py:9
  481.9 208.5 %all-reduce.19.cloned.1.call-start = ((), (), s32[]{:S(2)}) async-start(), calls=%async_computation.9 | async-start | bytes 2097152 | tf_op jit(solution)/shard_map/psum | solution.py:9
  704.0 95.8 %all-to-all-start.3 = ((bf16[8,256,512]{2,1,0:T(8,128)(2,1)}), bf16[8,256,512]{2,1,0:T(8,128)(2,1)S(1)}, u32[]{:S(2)}, u32[]{:S(2)}) async-start(bf16[8,256,512]{2,1,0:T(8,128)(2,1)} %stack.11), calls=%async_computation.3 | async-start | bytes 4194304 | tf_op jit(solution)/shard_map/all_to_all | solution.py:44
  710.7 83.9 %all-reduce.21.cloned.1.call-start = ((), (), s32[]{:S(2)}) async-start(), calls=%async_computation.10 | async-start | bytes 524288 | tf_op jit(solution)/shard_map/psum | solution.py:9
  711.5 212.0 %all-reduce.23.cloned.1.call-start = ((), (), s32[]{:S(2)}) async-start(), calls=%async_computation.11 | async-start | bytes 2097152 | tf_op jit(solution)/shard_map/psum | solution.py:9
Sparse Core Ops, SparseCore 0:
  24.6 82.5 all-reduce.8
  113.5 118.9 all-reduce.10
  255.9 80.7 all-reduce.12
  346.7 118.8 all-reduce.14
  484.1 81.1 all-reduce.16
  571.5 118.8 all-reduce.18
  713.9 80.7 all-reduce.20
  804.6 118.8 all-reduce.22
